TPU v7x, 256 devices: a whole 4x4x8 slice. The times are simulated.
256 devices in a mesh: tm: 16 (over x, y), space: 16 (over z, core).
Axes of the slice: x: 4, y: 4, z: 8, core: 2. Of those that a mesh axis runs over, the one named last changes fastest.
Arguments:
- fields: bfloat16 [16384, 2, 32768], P('tm', None, 'space')
- calendar_day: int32 [16384], P('tm'), may hold values from 0 to 364, as said below
- events: int32 [16, 96], replicated, may hold values from 0 to 16368, as said below
- lag_offsets: int32 [16], replicated, may hold values from 0 to 15, each once
Outputs:
- composite: float32 [16, 16, 2, 32768], P('tm', None, None, 'space')
Inputs may be any that keep to these rules, and one draw needn't show every extreme that they name: `calendar_day`: days of the year of successive record days, one or two calendar days apart. `events`: each entry is a record day; a day may repeat within a type. `lag_offsets`: each of 0 to 15 once.
All inputs are finite; a program needn't handle non-finite values.
Results may differ from a plain program's by a relative error of at most 0.0012.
Values may be sent and summed in bfloat16 or wider, within the bound.
No kernel may reach another device: no remote copies, remote signals or barrier semaphores. Data moves between devices by JAX's collectives and lax.ppermute only.
A program may use at most 64 MiB of HBM per device.

v0:
```python
import jax
import jax.numpy as jnp
from jax import lax
from jax.experimental import pallas as pl
from jax.experimental.pallas import tpu as pltpu
from jax.sharding import PartitionSpec as P

HARMONICS = 4
TWO_PI = 6.283185307179586
TERMS = 2 * HARMONICS + 1
SIDE = 4
TILE = 16
EXTRA = 128
CODE = 32
MERGE_VMEM, PRODUCTS_VMEM = 8 << 20, 24 << 20
CHUNK = 512
TOP = 32767.0
SECOND = 65534.0
F32 = jnp.float32
BF16 = jnp.bfloat16


def iota(shape, axis):
    return lax.broadcasted_iota(jnp.int32, shape, axis)


def dot(a, b):
    return jnp.dot(a, b, preferred_element_type=F32)


def dot_nt(a, b):
    return lax.dot_general(a, b, (((1,), (1,)), ((), ())), preferred_element_type=F32)


def design_rows(days):
    count = days.shape[1]
    phases = days.astype(F32) * (TWO_PI / 365.25)
    row = iota((TILE, count), 0)
    angles = ((row + 1) // 2).astype(F32) * phases
    waves = jnp.where(row % 2 == 1, jnp.cos(angles), jnp.sin(angles))
    rows = jnp.where(row == 0, 1.0, jnp.where(row < TERMS, waves, 0.0))
    return rows.astype(BF16)


def left_factor(me, events_ref, days_ref, left_ref):
    types, members = events_ref.shape
    lags = TILE
    local_days = days_ref.shape[1]
    rows = types * lags
    window = local_days + 128
    events = events_ref[...] - (me * local_days - 128)
    spot = iota((types, window), 1)
    histogram = jnp.zeros((types, window), F32)
    for m in range(members):
        histogram = histogram + jnp.where(events[:, m : m + 1] == spot, 1.0, 0.0)
    counts = jnp.concatenate(
        [histogram[:, 128 - o : 128 - o + local_days].astype(BF16) for o in range(lags)], axis=0
    )
    design = design_rows(days_ref[...])
    out_row = iota((rows, rows), 0)
    in_row = iota((rows, rows), 1)
    first, second, lag = out_row // (SIDE * lags), out_row // lags % SIDE, out_row % lags
    for v in range(2):
        rank = first * SIDE + second if v == 0 else second * SIDE + first
        order = (in_row == lag * types + (rank ^ me)).astype(F32).astype(BF16)
        spread = (iota((128, 256), 1) == 2 * iota((128, 256), 0) + v).astype(F32).astype(BF16)
        top = v * (rows + TILE)
        ordered = dot(order, counts).astype(BF16)
        for b in range(local_days // 128):
            day = slice(128 * b, 128 * b + 128)
            to = slice(256 * b, 256 * b + 256)
            left_ref[top : top + rows, to] = dot(ordered[:, day], spread).astype(BF16)
            left_ref[top + rows : top + rows + TILE, to] = dot(design[:, day], spread).astype(BF16)


def lane_sum(block):
    parts = [block[:, c : c + 128] for c in range(0, block.shape[1], 128)]
    while len(parts) > 1:
        parts = [x + y for x, y in zip(parts[::2], parts[1::2])] + parts[len(parts) & ~1 :]
    return parts[0]


def to_words(value, unit):
    scaled = value * unit
    high = jnp.round(scaled)
    return high, jnp.round((scaled - high) * SECOND)


def row_unit(code):
    return jnp.exp2(code * (-1.0 / 16.0)) * TOP


def row_code(value):
    peak = jnp.max(jnp.abs(value), axis=1, keepdims=True)
    return jnp.ceil(16.0 * jnp.log2(jnp.maximum(peak, 1e-30))) + 1.0


def to_int16(value):
    return value.astype(jnp.int32).astype(jnp.int16)


def encode(out, main, aux, members, total_days):
    rows, points = main.shape[0], main.shape[1] - EXTRA
    lane = iota((1, EXTRA), 1)

    def extra(block, code, unit):
        high, low = to_words(block, unit)
        low = jnp.where((lane >= TILE) & (lane < 2 * TILE), pltpu.roll(low, TILE, 1), 0.0)
        return to_int16(jnp.where(lane < TILE, high, low) + jnp.where(lane == CODE, code, 0.0))

    constant = aux[0:1, :points]
    mean = constant / aux[0:1, points : points + 1]
    centred = main[:, :points] - main[:, points : points + 1] * mean
    code = row_code(centred)
    out[:rows, :points] = to_int16(jnp.round(centred * row_unit(code)))
    out[:rows, points:] = extra(main[:, points:], code, TOP / members)
    row = iota((TILE, 1), 0)
    harmonic = aux[:, :points] - aux[:, points : points + 1] * mean
    harmonic = jnp.where(row == 0, constant, harmonic)
    code = row_code(harmonic)
    high, low = to_words(constant, row_unit(code[0:1]))
    words = jnp.where(row == 0, high, jnp.round(harmonic * row_unit(code)))
    out[rows:, :points] = to_int16(jnp.where(row == TERMS, low, words))
    out[rows:, points:] = extra(aux[:, points:], code, TOP / total_days)


def decode(message, members, total_days):
    rows, points = message.shape[0] - TILE, message.shape[1] - EXTRA
    lane = iota((1, EXTRA), 1)

    def extra(block, unit):
        words = block + pltpu.roll(block, EXTRA - TILE, 1) * (1.0 / SECOND)
        return jnp.where(lane < TILE, words * (1.0 / unit), 0.0)

    def values(block):
        block = block.astype(jnp.int32).astype(F32)
        code = block[:, points + CODE : points + CODE + 1]
        return block[:, :points], block[:, points:], jnp.exp2(code * (1.0 / 16.0)) * (1.0 / TOP)

    words, behind, step = values(message[rows:])
    low_side = extra(behind, TOP / total_days)
    constant = (words[0:1] + words[TERMS : TERMS + 1] * (1.0 / SECOND)) * step[0:1]
    mean = constant / low_side[0:1, 0:1]
    row = iota((TILE, 1), 0)
    aux = words * step + low_side[:, 0:1] * mean
    aux = jnp.where(row == 0, constant, jnp.where(row < TERMS, aux, 0.0))
    words, behind, step = values(message[:rows])
    side = extra(behind, TOP / members)
    return words * step + side[:, 0:1] * mean, side, aux, low_side


def products_kernel(total_days, me_ref, events_ref, days_ref, fields_ref, *refs):
    outs, sums_ref = refs[:-8], refs[-8]
    record_ref, left_ref, all_ref, part_ref, own_events, own_days, arrived = refs[-7:]
    members = events_ref.shape[1]
    points = fields_ref.shape[2]
    group = outs[0].shape[0] - TILE
    rows = SIDE * group
    half = rows + TILE
    chunks = [slice(c, c + CHUNK) for c in range(0, points, CHUNK)]
    copies = [
        pltpu.make_async_copy(fields_ref.at[:, :, c], record_ref.at[:, :, c], arrived.at[i])
        for i, c in enumerate(chunks)
    ]
    small = [
        pltpu.make_async_copy(events_ref, own_events, arrived.at[len(chunks)]),
        pltpu.make_async_copy(days_ref, own_days, arrived.at[len(chunks) + 1]),
    ]
    for copy in small + copies:
        copy.start()
    for copy in small:
        copy.wait()
    left_factor(me_ref[0], own_events, own_days, left_ref)
    for v in range(2):
        left = left_ref[v * half : (v + 1) * half, :]
        pad = jnp.zeros((EXTRA - TILE, left.shape[1]), BF16)
        all_ref[v * half : (v + 1) * half, points:] = dot_nt(
            left, jnp.concatenate([left[rows:, :], pad], axis=0)
        )
    record = record_ref.reshape(2 * record_ref.shape[0], points)
    for copy, c in zip(copies, chunks):
        copy.wait()
        all_ref[:, c] = dot(left_ref[...], record[:, c])
    for r in (2, 1, 3, 0):
        for v in range(2):
            top = v * half + group * r
            out = outs[SIDE * v + r]
            if r:
                main = all_ref[top : top + group, :]
                aux = all_ref[v * half + rows : (v + 1) * half, :]
                encode(out, main, aux, members, total_days)
            else:
                out[:group, :] = all_ref[top : top + group, :]
                out[group:, :] = all_ref[v * half + rows : (v + 1) * half, :]
    for i in range(SIDE * SIDE):
        for v in range(2):
            place = i if v == 0 else i % SIDE * SIDE + i // SIDE
            top = v * half + TILE * place
            part_ref[2 * TILE * i + TILE * v : 2 * TILE * i + TILE * (v + 1), :] = lane_sum(
                all_ref[top : top + TILE, :points]
            )
    design = [lane_sum(all_ref[v * half + rows : (v + 1) * half, :points]) for v in range(2)]
    types = [
        part_ref[pl.ds(pl.multiple_of((e ^ me_ref[0]) * 2 * TILE, 2 * TILE), 2 * TILE), :]
        for e in range(SIDE * SIDE)
    ]
    totals = lax.dot_general(
        jnp.ones((8, 128), F32),
        jnp.concatenate(types + design, axis=0),
        (((1,), (1,)), ((), ())),
        precision=lax.Precision.HIGHEST,
        preferred_element_type=F32,
    )
    count = 2 * TILE
    last = totals[0:1, count * SIDE * SIDE :]
    for e in range(SIDE * SIDE):
        line = [totals[0:1, count * e : count * (e + 1)], last, jnp.zeros((1, 128 - 2 * count), F32)]
        sums_ref[e : e + 1, :] = jnp.concatenate(line, axis=1)


def vmem():
    return pl.BlockSpec(memory_space=pltpu.VMEM)


def products(me, events, days, fields):
    local_days, _, points = fields.shape
    types = events.shape[0]
    group = types * TILE // SIDE
    half = types * TILE + TILE
    columns = points + EXTRA
    kept = jax.ShapeDtypeStruct((group + TILE, columns), F32)
    message = jax.ShapeDtypeStruct((group + TILE, columns), jnp.int16)
    tm = lax.axis_size("tm")
    sums = jax.ShapeDtypeStruct((tm, 128), F32)
    return pl.pallas_call(
        lambda *refs: products_kernel(local_days * tm, *refs),
        in_specs=[
            pl.BlockSpec(memory_space=pltpu.SMEM),
            pl.BlockSpec(memory_space=pltpu.HBM),
            pl.BlockSpec(memory_space=pltpu.HBM),
            pl.BlockSpec(memory_space=pltpu.HBM),
        ],
        out_specs=[vmem()] * (2 * SIDE + 1),
        out_shape=([kept] + [message] * (SIDE - 1)) * 2 + [sums],
        scratch_shapes=[
            pltpu.VMEM(fields.shape, BF16),
            pltpu.VMEM((2 * half, 2 * local_days), BF16),
            pltpu.VMEM((2 * half, columns), F32),
            pltpu.VMEM((2 * types * TILE, 128), F32),
            pltpu.VMEM(events.shape, jnp.int32),
            pltpu.VMEM((1, local_days), jnp.int32),
            pltpu.SemaphoreType.DMA((points // CHUNK + 2,)),
        ],
        compiler_params=pltpu.CompilerParams(vmem_limit_bytes=PRODUCTS_VMEM),
        name="products",
    )(me, *(pltpu.with_memory_space_constraint(x, pltpu.HBM) for x in (events, days.reshape(1, local_days), fields)))


def added(taken, members, total_days):
    rows, points = taken[0].shape[0] - TILE, taken[0].shape[1] - EXTRA
    kept = taken[0]
    main, side = kept[:rows, :points], kept[:rows, points:]
    aux, low_side = kept[rows:, :points], kept[rows:, points:]
    for t in taken[1:]:
        a, b, c, d = decode(t, members, total_days)
        main, side, aux, low_side = main + a, side + b, aux + c, low_side + d
    main = jnp.concatenate([main, side], axis=1)
    aux = jnp.concatenate([aux, low_side], axis=1)
    return main, aux


def merge_kernel(members, total_days, *refs):
    taken, outs = refs[:SIDE], refs[SIDE:]
    main, aux = added(taken, members, total_days)
    for r in (2, 1, 3):
        encode(outs[r], main[TILE * r : TILE * (r + 1)], aux, members, total_days)
    outs[0][:TILE, :] = main[:TILE]
    outs[0][TILE:, :] = aux


def merge(taken, members, total_days):
    columns = taken[0].shape[1]
    kept = jax.ShapeDtypeStruct((2 * TILE, columns), F32)
    message = jax.ShapeDtypeStruct((2 * TILE, columns), jnp.int16)
    return pl.pallas_call(
        lambda *refs: merge_kernel(members, total_days, *refs),
        in_specs=[vmem()] * SIDE,
        out_specs=[vmem()] * SIDE,
        out_shape=[kept] + [message] * (SIDE - 1),
        compiler_params=pltpu.CompilerParams(vmem_limit_bytes=MERGE_VMEM),
        name="merge",
    )(*taken)


def finish_kernel(members, total_days, all_points, lags_ref, sums_ref, *refs):
    taken, (maps_ref, rows_ref) = refs[: 2 * SIDE], refs[2 * SIDE :]
    lags, _, points = maps_ref.shape
    sums = jnp.sum(sums_ref[...], axis=0, keepdims=True)
    for v in range(2):
        total = jnp.concatenate(added(taken[SIDE * v : SIDE * (v + 1)], members, total_days), axis=0)
        row, lane = iota((2 * TILE, 1), 0), iota((1, EXTRA), 1)
        place = jnp.where(row < TILE, row + TILE * v, row + TILE * (v + 1))
        over = jnp.where(iota((1, 128), 1) == place, sums, 0.0)
        over = jnp.sum(over, axis=1, keepdims=True)
        side = jnp.where(lane == CODE, over, total[:, points:])
        total = jnp.concatenate([total[:, :points], side], axis=1)
        for k in range(TERMS):
            pivot = total[TILE + k : TILE + k + 1, :]
            column = points + k
            factor = total[:, column : column + 1] / pivot[:, column : column + 1]
            factor = jnp.where((row < TILE) | (row > TILE + k), factor, 0.0)
            total = total - factor * pivot
        column = points + CODE
        mean = total[:TILE, column : column + 1] / all_points
        rows_ref[...] = (total[:TILE, :points] - mean) / members
        for l in range(lags):
            maps_ref[l, v : v + 1, :] = rows_ref[pl.ds(lags_ref[l], 1), :]


def finish(members, total_days, all_points, lag_offsets, sums, taken):
    points = taken[0].shape[1] - EXTRA
    lags = lag_offsets.shape[0]
    return pl.pallas_call(
        lambda *refs: finish_kernel(members, total_days, all_points, *refs),
        in_specs=[pl.BlockSpec(memory_space=pltpu.SMEM)] + [vmem()] * (2 * SIDE + 1),
        scratch_shapes=[pltpu.VMEM((TILE, points), F32)],
        out_shape=jax.ShapeDtypeStruct((lags, 2, points), F32),
        compiler_params=pltpu.CompilerParams(vmem_limit_bytes=MERGE_VMEM),
        name="finish",
    )(lag_offsets, sums, *taken)


def swap(value, axis, mask):
    return lax.ppermute(value, axis, [(i, i ^ mask) for i in range(lax.axis_size(axis))])


def map_sums(sums):
    types, space = sums.shape[0], lax.axis_size("space")
    chips = space // 2
    sums = jnp.broadcast_to(sums[:, None], (types, chips, sums.shape[1]))
    groups = [[2 * i + core for i in range(types * chips)] for core in range(2)]
    return lax.all_to_all(
        sums.reshape(types * chips, -1), ("tm", "space"), 0, 0, axis_index_groups=groups, tiled=True
    )


def shards(fields, calendar_day, events, lag_offsets):
    me = lax.axis_index("tm").astype(jnp.int32).reshape(1)
    members = events.shape[1]
    total_days = fields.shape[0] * lax.axis_size("tm")
    all_points = fields.shape[2] * lax.axis_size("space")
    *sent, sums = products(me, events, calendar_day, fields)
    sent, sums = lax.optimization_barrier((sent, sums + swap(sums, "space", 1)))
    mine = [[sent[0]] + [None] * 3, [sent[SIDE]] + [None] * 3]
    for r in (2, 1, 3):
        mine[0][r] = swap(sent[r], "tm", SIDE * r)
        mine[1][r] = swap(sent[SIDE + r], "tm", r)
    sums = map_sums(sums)
    taken = []
    for v in range(2):
        parts = merge(mine[v], members, total_days)
        taken += [parts[0]] + [swap(parts[r], "tm", r if v == 0 else SIDE * r) for r in (1, 2, 3)]
    return finish(members, total_days, all_points, lag_offsets, sums, taken)[None]


def solution(mesh):
    return jax.shard_map(
        shards,
        mesh=mesh,
        in_specs=(P("tm", None, "space"), P("tm"), P(), P()),
        out_specs=P("tm", None, None, "space"),
        check_vma=False,
    )
```

profile of v0, /device:TPU:8, one launch (start us, length us, event | category | flops | bytes accessed | tf_op | source)
XLA Modules:
  0.0 77.8 jit_solution(8351083963520357099)
XLA Ops:
  0.0 0.0 copy-start
  0.0 10.2 %products.1 = (f32[80,2176]{1,0:T(8,128)S(1)}, s16[80,2176]{1,0:T(8,128)(2,1)S(1)}, s16[80,2176]{1,0:T(8,128)(2,1)S(1)}, s16[80,2176]{1,0:T(8,128)(2,1)S(1)}, f3...) custom-call(s32[1]{0:T(128)} %bitcast.refs_0_, ...), custom_call_target="tpu_custom_call" | custom-call | tf_op jit(solution)/shard_map/products/pallas_call | solution.py:235
  10.2 0.1 collective-permute-start
  10.3 1.2 %collective-permute-done = f32[16,128]{1,0:T(8,128)S(1)} collective-permute-done((f32[16,128]{1,0:T(8,128)S(1)}, f32[16,128]{1,0:T(8,128)S(1)}, u32[]{:S(2)}, u32[]{:S(2)}) %collective-permute-start) | collective-permute-done | bytes 8224 | tf_op jit(solution)/shard_map/ppermute | solution.py:334
  11.5 2.2 %collective-permute-start.7 = (s16[80,2176]{1,0:T(8,128)(2,1)S(1)}, s16[80,2176]{1,0:T(8,128)(2,1)S(1)}, u32[]{:S(2)}, u32[]{:S(2)}) collective-permute-start(s16[80,2176]{1,0:T(8,128)(2,1)S(1)} %get-tuple-element.50), channel_id=1, source_target_pairs={{0,16},{16,0},{32,48},{48,32},{64,80},{80,64},{96,112},{112,96},{1... | collective-permute-start | bytes 1044488 | tf_op jit(solution)/shard_map/ppermute | solution.py:334
  13.6 0.9 %collective-permute-start.8 = (s16[80,2176]{1,0:T(8,128)(2,1)S(1)}, s16[80,2176]{1,0:T(8,128)(2,1)S(1)}, u32[]{:S(2)}, u32[]{:S(2)}) collective-permute-start(s16[80,2176]{1,0:T(8,128)(2,1)S(1)} %get-tuple-element.51), channel_id=1, source_target_pairs={{0,32},{16,48},{32,0},{48,16},{64,96},{80,112},{96,64},{112,80},{1... | collective-permute-start | bytes 1044488 | tf_op jit(solution)/shard_map/ppermute | solution.py:334
  14.5 0.6 collective-permute-start.9
  15.1 1.4 %collective-permute-start.1 = (s16[80,2176]{1,0:T(8,128)(2,1)S(1)}, s16[80,2176]{1,0:T(8,128)(2,1)S(1)}, u32[]{:S(2)}, u32[]{:S(2)}) collective-permute-start(s16[80,2176]{1,0:T(8,128)(2,1)S(1)} %get-tuple-element.42), channel_id=1, source_target_pairs={{0,64},{16,80},{32,96},{48,112},{64,0},{80,16},{96,32},{112,48},{1... | collective-permute-start | bytes 1044488 | tf_op jit(solution)/shard_map/ppermute | solution.py:334
  16.5 2.7 %collective-permute-start.2 = (s16[80,2176]{1,0:T(8,128)(2,1)S(1)}, s16[80,2176]{1,0:T(8,128)(2,1)S(1)}, u32[]{:S(2)}, u32[]{:S(2)}) collective-permute-start(s16[80,2176]{1,0:T(8,128)(2,1)S(1)} %get-tuple-element.43), channel_id=1, source_target_pairs={{0,128},{16,144},{32,160},{48,176},{64,192},{80,208},{96,224},{112... | collective-permute-start | bytes 1044488 | tf_op jit(solution)/shard_map/ppermute | solution.py:334
  19.2 3.4 %collective-permute-done.7.refs_1_ = s16[80,2176]{1,0:T(8,128)(2,1)S(1)} collective-permute-done((s16[80,2176]{1,0:T(8,128)(2,1)S(1)}, s16[80,2176]{1,0:T(8,128)(2,1)S(1)}, u32[]{:S(2)}, u32[]{:S(2)}) %collective-permute-start.7) | collective-permute-done | bytes 348192 | tf_op jit(solution)/shard_map/ppermute | solution.py:334
  22.6 2.6 %collective-permute-start.3 = (s16[80,2176]{1,0:T(8,128)(2,1)S(1)}, s16[80,2176]{1,0:T(8,128)(2,1)S(1)}, u32[]{:S(2)}, u32[]{:S(2)}) collective-permute-start(s16[80,2176]{1,0:T(8,128)(2,1)S(1)} %get-tuple-element.44), channel_id=1, source_target_pairs={{0,192},{16,208},{32,224},{48,240},{64,128},{80,144},{96,160},{112... | collective-permute-start | bytes 1044488 | tf_op jit(solution)/shard_map/ppermute | solution.py:334
  25.3 5.0 %collective-permute-done.8.refs_2_ = s16[80,2176]{1,0:T(8,128)(2,1)S(1)} collective-permute-done((s16[80,2176]{1,0:T(8,128)(2,1)S(1)}, s16[80,2176]{1,0:T(8,128)(2,1)S(1)}, u32[]{:S(2)}, u32[]{:S(2)}) %collective-permute-start.8) | collective-permute-done | bytes 348192 | tf_op jit(solution)/shard_map/ppermute | solution.py:334
  30.3 1.4 %collective-permute-done.9.refs_3_ = s16[80,2176]{1,0:T(8,128)(2,1)S(1)} collective-permute-done((s16[80,2176]{1,0:T(8,128)(2,1)S(1)}, s16[80,2176]{1,0:T(8,128)(2,1)S(1)}, u32[]{:S(2)}, u32[]{:S(2)}) %collective-permute-start.9) | collective-permute-done | bytes 348192 | tf_op jit(solution)/shard_map/ppermute | solution.py:334
  31.6 0.7 merge.3
  32.4 1.8 %collective-permute-start.10 = (s16[32,2176]{1,0:T(8,128)(2,1)S(1)}, s16[32,2176]{1,0:T(8,128)(2,1)S(1)}, u32[]{:S(2)}, u32[]{:S(2)}) collective-permute-start(s16[32,2176]{1,0:T(8,128)(2,1)S(1)} %get-tuple-element.54), channel_id=1, source_target_pairs={{0,64},{16,80},{32,96},{48,112},{64,0},{80,16},{96,32},{112,48},{1... | collective-permute-start | bytes 417800 | tf_op jit(solution)/shard_map/ppermute | solution.py:334
  34.1 2.7 %collective-permute-start.11 = (s16[32,2176]{1,0:T(8,128)(2,1)S(1)}, s16[32,2176]{1,0:T(8,128)(2,1)S(1)}, u32[]{:S(2)}, u32[]{:S(2)}) collective-permute-start(s16[32,2176]{1,0:T(8,128)(2,1)S(1)} %get-tuple-element.55), channel_id=1, source_target_pairs={{0,128},{16,144},{32,160},{48,176},{64,192},{80,208},{96,224},{112... | collective-permute-start | bytes 417800 | tf_op jit(solution)/shard_map/ppermute | solution.py:334
  36.9 0.0 collective-permute-done.1.refs_1_
  36.9 0.5 collective-permute-start.12
  37.3 0.0 collective-permute-done.2.refs_2_
  37.3 6.7 %collective-permute-done.3.refs_3_ = s16[80,2176]{1,0:T(8,128)(2,1)S(1)} collective-permute-done((s16[80,2176]{1,0:T(8,128)(2,1)S(1)}, s16[80,2176]{1,0:T(8,128)(2,1)S(1)}, u32[]{:S(2)}, u32[]{:S(2)}) %collective-permute-start.3) | collective-permute-done | bytes 348192 | tf_op jit(solution)/shard_map/ppermute | solution.py:334
  44.1 0.7 merge.2
  44.8 1.5 %collective-permute-start.4 = (s16[32,2176]{1,0:T(8,128)(2,1)S(1)}, s16[32,2176]{1,0:T(8,128)(2,1)S(1)}, u32[]{:S(2)}, u32[]{:S(2)}) collective-permute-start(s16[32,2176]{1,0:T(8,128)(2,1)S(1)} %get-tuple-element.46), channel_id=1, source_target_pairs={{0,16},{16,0},{32,48},{48,32},{64,80},{80,64},{96,112},{112,96},{1... | collective-permute-start | bytes 417800 | tf_op jit(solution)/shard_map/ppermute | solution.py:334
  46.3 1.5 %collective-permute-start.5 = (s16[32,2176]{1,0:T(8,128)(2,1)S(1)}, s16[32,2176]{1,0:T(8,128)(2,1)S(1)}, u32[]{:S(2)}, u32[]{:S(2)}) collective-permute-start(s16[32,2176]{1,0:T(8,128)(2,1)S(1)} %get-tuple-element.47), channel_id=1, source_target_pairs={{0,32},{16,48},{32,0},{48,16},{64,96},{80,112},{96,64},{112,80},{1... | collective-permute-start | bytes 417800 | tf_op jit(solution)/shard_map/ppermute | solution.py:334
  47.8 0.0 collective-permute-done.10.refs_7_
  47.8 0.5 collective-permute-start.6
  48.4 26.4 %all_to_all.11 = f32[128,1,128]{2,1,0:T(1,128)S(1)} all-to-all(f32[128,1,128]{2,1,0:T(1,128)S(1)} %bitcast.6), channel_id=1, replica_groups={{0,2,4,6,8,10,12,14,16,18,20,22,24,26,28,30,32,34,36,38,40,42,44,46,48,..., dimensions={0} | all-to-all | bytes 131072 | tf_op jit(solution)/shard_map/all_to_all | solution.py:342
  74.8 0.0 collective-permute-done.11.refs_8_
  74.8 0.0 collective-permute-done.12.refs_9_
  74.8 0.0 collective-permute-done.4.refs_3_
  74.8 0.0 collective-permute-done.5.refs_4_
  74.8 0.0 collective-permute-done.6.refs_5_
  74.8 0.0 copy-done
  74.8 3.0 %finish.1 = f32[16,2,2048]{2,1,0:T(2,128)} custom-call(s32[16]{0:T(128)S(1)} %copy-done, f32[128,128]{1,0:T(8,128)S(1)} %bitcast.5, f32[32,2176]{1,0:T(8,128)S(1)} %get-tuple-element.45.refs_2_, s16[32,2176]{1,0:T(8,128)(2,1)S(1)} %collective-permute-done.4.refs_3_, s16[32,2176]{1,0:T(8,128)(2,1)S(1)} %collective-permute-done.5.refs_4_, ...), custom_call_target="tpu_custom_call" | custom-call | tf_op jit(solution)/shard_map/finish/pallas_call | solution.py:323
  (2 shorter events, 0.0 us)
Async XLA Ops:
  0.0 74.8 %copy-start = (s32[16]{0:T(128)S(1)}, s32[16]{0:T(128)}, u32[]{:S(2)}) copy-start(s32[16]{0:T(128)} %refs_0_.1) | copy-start | bytes 196
  10.2 1.3 %collective-permute-start = (f32[16,128]{1,0:T(8,128)S(1)}, f32[16,128]{1,0:T(8,128)S(1)}, u32[]{:S(2)}, u32[]{:S(2)}) collective-permute-start(f32[16,128]{1,0:T(8,128)S(1)} %get-tuple-element.39), channel_id=1, source_target_pairs={{0,1},{1,0},{2,3},{3,2},{4,5},{5,4},{6,7},{7,6},{8,9},{9,8},{10,11... | collective-permute-start | bytes 24584 | tf_op jit(solution)/shard_map/ppermute | solution.py:334
  11.5 11.2 %collective-permute-start.7 = (s16[80,2176]{1,0:T(8,128)(2,1)S(1)}, s16[80,2176]{1,0:T(8,128)(2,1)S(1)}, u32[]{:S(2)}, u32[]{:S(2)}) collective-permute-start(s16[80,2176]{1,0:T(8,128)(2,1)S(1)} %get-tuple-element.50), channel_id=1, source_target_pairs={{0,16},{16,0},{32,48},{48,32},{64,80},{80,64},{96,112},{112,96},{1... | collective-permute-start | bytes 1044488 | tf_op jit(solution)/shard_map/ppermute | solution.py:334
  13.6 16.6 %collective-permute-start.8 = (s16[80,2176]{1,0:T(8,128)(2,1)S(1)}, s16[80,2176]{1,0:T(8,128)(2,1)S(1)}, u32[]{:S(2)}, u32[]{:S(2)}) collective-permute-start(s16[80,2176]{1,0:T(8,128)(2,1)S(1)} %get-tuple-element.51), channel_id=1, source_target_pairs={{0,32},{16,48},{32,0},{48,16},{64,96},{80,112},{96,64},{112,80},{1... | collective-permute-start | bytes 1044488 | tf_op jit(solution)/shard_map/ppermute | solution.py:334
  14.5 17.1 %collective-permute-start.9 = (s16[80,2176]{1,0:T(8,128)(2,1)S(1)}, s16[80,2176]{1,0:T(8,128)(2,1)S(1)}, u32[]{:S(2)}, u32[]{:S(2)}) collective-permute-start(s16[80,2176]{1,0:T(8,128)(2,1)S(1)} %get-tuple-element.52), channel_id=1, source_target_pairs={{0,48},{16,32},{32,16},{48,0},{64,112},{80,96},{96,80},{112,64},{1... | collective-permute-start | bytes 1044488 | tf_op jit(solution)/shard_map/ppermute | solution.py:334
  15.1 21.8 %collective-permute-start.1 = (s16[80,2176]{1,0:T(8,128)(2,1)S(1)}, s16[80,2176]{1,0:T(8,128)(2,1)S(1)}, u32[]{:S(2)}, u32[]{:S(2)}) collective-permute-start(s16[80,2176]{1,0:T(8,128)(2,1)S(1)} %get-tuple-element.42), channel_id=1, source_target_pairs={{0,64},{16,80},{32,96},{48,112},{64,0},{80,16},{96,32},{112,48},{1... | collective-permute-start | bytes 1044488 | tf_op jit(solution)/shard_map/ppermute | solution.py:334
  16.5 20.9 %collective-permute-start.2 = (s16[80,2176]{1,0:T(8,128)(2,1)S(1)}, s16[80,2176]{1,0:T(8,128)(2,1)S(1)}, u32[]{:S(2)}, u32[]{:S(2)}) collective-permute-start(s16[80,2176]{1,0:T(8,128)(2,1)S(1)} %get-tuple-element.43), channel_id=1, source_target_pairs={{0,128},{16,144},{32,160},{48,176},{64,192},{80,208},{96,224},{112... | collective-permute-start | bytes 1044488 | tf_op jit(solution)/shard_map/ppermute | solution.py:334
  22.6 21.4 %collective-permute-start.3 = (s16[80,2176]{1,0:T(8,128)(2,1)S(1)}, s16[80,2176]{1,0:T(8,128)(2,1)S(1)}, u32[]{:S(2)}, u32[]{:S(2)}) collective-permute-start(s16[80,2176]{1,0:T(8,128)(2,1)S(1)} %get-tuple-element.44), channel_id=1, source_target_pairs={{0,192},{16,208},{32,224},{48,240},{64,128},{80,144},{96,160},{112... | collective-permute-start | bytes 1044488 | tf_op jit(solution)/shard_map/ppermute | solution.py:334
  32.4 15.5 %collective-permute-start.10 = (s16[32,2176]{1,0:T(8,128)(2,1)S(1)}, s16[32,2176]{1,0:T(8,128)(2,1)S(1)}, u32[]{:S(2)}, u32[]{:S(2)}) collective-permute-start(s16[32,2176]{1,0:T(8,128)(2,1)S(1)} %get-tuple-element.54), channel_id=1, source_target_pairs={{0,64},{16,80},{32,96},{48,112},{64,0},{80,16},{96,32},{112,48},{1... | collective-permute-start | bytes 417800 | tf_op jit(solution)/shard_map/ppermute | solution.py:334
  34.1 40.7 %collective-permute-start.11 = (s16[32,2176]{1,0:T(8,128)(2,1)S(1)}, s16[32,2176]{1,0:T(8,128)(2,1)S(1)}, u32[]{:S(2)}, u32[]{:S(2)}) collective-permute-start(s16[32,2176]{1,0:T(8,128)(2,1)S(1)} %get-tuple-element.55), channel_id=1, source_target_pairs={{0,128},{16,144},{32,160},{48,176},{64,192},{80,208},{96,224},{112... | collective-permute-start | bytes 417800 | tf_op jit(solution)/shard_map/ppermute | solution.py:334
  36.9 37.9 %collective-permute-start.12 = (s16[32,2176]{1,0:T(8,128)(2,1)S(1)}, s16[32,2176]{1,0:T(8,128)(2,1)S(1)}, u32[]{:S(2)}, u32[]{:S(2)}) collective-permute-start(s16[32,2176]{1,0:T(8,128)(2,1)S(1)} %get-tuple-element.56), channel_id=1, source_target_pairs={{0,192},{16,208},{32,224},{48,240},{64,128},{80,144},{96,160},{112... | collective-permute-start | bytes 417800 | tf_op jit(solution)/shard_map/ppermute | solution.py:334
  44.8 30.0 %collective-permute-start.4 = (s16[32,2176]{1,0:T(8,128)(2,1)S(1)}, s16[32,2176]{1,0:T(8,128)(2,1)S(1)}, u32[]{:S(2)}, u32[]{:S(2)}) collective-permute-start(s16[32,2176]{1,0:T(8,128)(2,1)S(1)} %get-tuple-element.46), channel_id=1, source_target_pairs={{0,16},{16,0},{32,48},{48,32},{64,80},{80,64},{96,112},{112,96},{1... | collective-permute-start | bytes 417800 | tf_op jit(solution)/shard_map/ppermute | solution.py:334
  46.3 28.5 %collective-permute-start.5 = (s16[32,2176]{1,0:T(8,128)(2,1)S(1)}, s16[32,2176]{1,0:T(8,128)(2,1)S(1)}, u32[]{:S(2)}, u32[]{:S(2)}) collective-permute-start(s16[32,2176]{1,0:T(8,128)(2,1)S(1)} %get-tuple-element.47), channel_id=1, source_target_pairs={{0,32},{16,48},{32,0},{48,16},{64,96},{80,112},{96,64},{112,80},{1... | collective-permute-start | bytes 417800 | tf_op jit(solution)/shard_map/ppermute | solution.py:334
  47.8 27.0 %collective-permute-start.6 = (s16[32,2176]{1,0:T(8,128)(2,1)S(1)}, s16[32,2176]{1,0:T(8,128)(2,1)S(1)}, u32[]{:S(2)}, u32[]{:S(2)}) collective-permute-start(s16[32,2176]{1,0:T(8,128)(2,1)S(1)} %get-tuple-element.48), channel_id=1, source_target_pairs={{0,48},{16,32},{32,16},{48,0},{64,112},{80,96},{96,80},{112,64},{1... | collective-permute-start | bytes 417800 | tf_op jit(solution)/shard_map/ppermute | solution.py:334
where the time goes:
time: 77.9 us; the launch traced here: 77.8 us
  blocking collectives  26.4 us (34%)
  starting transfers between devices  19 us (24%)
  waiting for transfers between devices  17.7 us (23%)
  Pallas kernels  14.6 us (19%)
    all_to_all x1, blocking collectives, map_sums(): lax.all_to_all(sums.reshape(types * chips, -1), ('tm', 'space'), 0, 0, ax...  26.4 us
    ppermute x13, starting transfers between devices, swap(): lax.ppermute(value, axis, [(i, i ^ mask) for i in range(lax.axis_size(axi...  19 us
    ppermute x13, waiting for transfers between devices, swap(): lax.ppermute(value, axis, [(i, i ^ mask) for i in range(lax.axis_size(axi...  17.7 us
    pallas_call x1, Pallas kernels, products(): pl.pallas_call(lambda *refs: products_kernel(local_days * tm, *refs), in_...  10.2 us
    pallas_call x1, Pallas kernels, finish(): pl.pallas_call(lambda *refs: finish_kernel(members, total_days, all_point...  2.97 us
  transfers between devices with their start and end apart: 13, of which 5 were waited for; matrix products, arithmetic and copies ran while one was open for 0% of the time, Pallas kernels for 2%

commit v1 on v0

--- a/solution.py
+++ b/solution.py
@@ -18,6 +18,14 @@
 SECOND = 65534.0
 F32 = jnp.float32
 BF16 = jnp.bfloat16
+
+
+def near(rank):
+    return (rank & 1) * 4 + (rank >> 1)
+
+
+def far(rank):
+    return (rank & 1) * 12 + (rank >> 1) * 3
 
 
 def iota(shape, axis):
@@ -61,7 +69,7 @@
     in_row = iota((rows, rows), 1)
     first, second, lag = out_row // (SIDE * lags), out_row // lags % SIDE, out_row % lags
     for v in range(2):
-        rank = first * SIDE + second if v == 0 else second * SIDE + first
+        rank = near(first) ^ far(second) if v == 0 else far(first) ^ near(second)
         order = (in_row == lag * types + (rank ^ me)).astype(F32).astype(BF16)
         spread = (iota((128, 256), 1) == 2 * iota((128, 256), 0) + v).astype(F32).astype(BF16)
         top = v * (rows + TILE)
@@ -200,10 +208,12 @@
                 all_ref[top : top + TILE, :points]
             )
     design = [lane_sum(all_ref[v * half + rows : (v + 1) * half, :points]) for v in range(2)]
-    types = [
-        part_ref[pl.ds(pl.multiple_of((e ^ me_ref[0]) * 2 * TILE, 2 * TILE), 2 * TILE), :]
-        for e in range(SIDE * SIDE)
-    ]
+    types = []
+    for e in range(SIDE * SIDE):
+        rank = e ^ me_ref[0]
+        high, mixed = rank & 10, rank ^ (rank >> 1)
+        place = (mixed & 1) * 8 + (mixed >> 2 & 1) * 4 + (high & 2) + (high >> 3)
+        types.append(part_ref[pl.ds(pl.multiple_of(place * 2 * TILE, 2 * TILE), 2 * TILE), :])
     totals = lax.dot_general(
         jnp.ones((8, 128), F32),
         jnp.concatenate(types + design, axis=0),
@@ -213,9 +223,11 @@
     )
     count = 2 * TILE
     last = totals[0:1, count * SIDE * SIDE :]
+    space = sums_ref.shape[0] // (SIDE * SIDE)
     for e in range(SIDE * SIDE):
         line = [totals[0:1, count * e : count * (e + 1)], last, jnp.zeros((1, 128 - 2 * count), F32)]
-        sums_ref[e : e + 1, :] = jnp.concatenate(line, axis=1)
+        line = jnp.broadcast_to(jnp.concatenate(line, axis=1), (space, 128))
+        sums_ref[space * e : space * (e + 1), :] = line
 
 
 def vmem():
@@ -231,7 +243,7 @@
     kept = jax.ShapeDtypeStruct((group + TILE, columns), F32)
     message = jax.ShapeDtypeStruct((group + TILE, columns), jnp.int16)
     tm = lax.axis_size("tm")
-    sums = jax.ShapeDtypeStruct((tm, 128), F32)
+    sums = jax.ShapeDtypeStruct((tm * lax.axis_size("space"), 128), F32)
     return pl.pallas_call(
         lambda *refs: products_kernel(local_days * tm, *refs),
         in_specs=[
@@ -292,56 +304,63 @@
     )(*taken)
 
 
-def finish_kernel(members, total_days, all_points, lags_ref, sums_ref, *refs):
-    taken, (maps_ref, rows_ref) = refs[: 2 * SIDE], refs[2 * SIDE :]
+def fold_kernel(v, members, total_days, *refs):
+    taken, rows_ref = refs[:SIDE], refs[SIDE]
+    total = jnp.concatenate(added(taken, members, total_days), axis=0)
+    points = total.shape[1] - EXTRA
+    row, lane = iota((2 * TILE, 1), 0), iota((1, EXTRA), 1)
+    unit = (lane == TILE * (v + 1) + row) & (row >= TILE) & (row < TILE + TERMS)
+    total = jnp.concatenate([total[:, :points], jnp.where(unit, 1.0, total[:, points:])], axis=1)
+    for k in range(TERMS):
+        pivot = total[TILE + k : TILE + k + 1, :]
+        column = points + k
+        factor = total[:, column : column + 1] / pivot[:, column : column + 1]
+        factor = jnp.where((row < TILE) | (row > TILE + k), factor, 0.0)
+        total = total - factor * pivot
+    rows_ref[...] = total[:TILE]
+
+
+def fold(v, taken, members, total_days):
+    return pl.pallas_call(
+        lambda *refs: fold_kernel(v, members, total_days, *refs),
+        in_specs=[vmem()] * SIDE,
+        out_specs=vmem(),
+        out_shape=jax.ShapeDtypeStruct((TILE, taken[0].shape[1]), F32),
+        compiler_params=pltpu.CompilerParams(vmem_limit_bytes=MERGE_VMEM),
+        name="fold",
+    )(*taken)
+
+
+def finish_kernel(members, all_points, lags_ref, sums_ref, *refs):
+    folded, maps_ref, rows_ref = refs[:2], refs[2], refs[3]
     lags, _, points = maps_ref.shape
     sums = jnp.sum(sums_ref[...], axis=0, keepdims=True)
+    row, lane = iota((TILE, 1), 0), iota((1, EXTRA), 1)
     for v in range(2):
-        total = jnp.concatenate(added(taken[SIDE * v : SIDE * (v + 1)], members, total_days), axis=0)
-        row, lane = iota((2 * TILE, 1), 0), iota((1, EXTRA), 1)
-        place = jnp.where(row < TILE, row + TILE * v, row + TILE * (v + 1))
-        over = jnp.where(iota((1, 128), 1) == place, sums, 0.0)
-        over = jnp.sum(over, axis=1, keepdims=True)
-        side = jnp.where(lane == CODE, over, total[:, points:])
-        total = jnp.concatenate([total[:, :points], side], axis=1)
-        for k in range(TERMS):
-            pivot = total[TILE + k : TILE + k + 1, :]
-            column = points + k
-            factor = total[:, column : column + 1] / pivot[:, column : column + 1]
-            factor = jnp.where((row < TILE) | (row > TILE + k), factor, 0.0)
-            total = total - factor * pivot
-        column = points + CODE
-        mean = total[:TILE, column : column + 1] / all_points
-        rows_ref[...] = (total[:TILE, :points] - mean) / members
+        rows = folded[v][...]
+        design = (lane >= TILE * (v + 2)) & (lane < TILE * (v + 3))
+        weights = jnp.where(lane == TILE * v + row, 1.0, jnp.where(design, rows[:, points:], 0.0))
+        mean = jnp.sum(weights * sums, axis=1, keepdims=True) / all_points
+        rows_ref[...] = (rows[:, :points] - mean) / members
         for l in range(lags):
             maps_ref[l, v : v + 1, :] = rows_ref[pl.ds(lags_ref[l], 1), :]
 
 
-def finish(members, total_days, all_points, lag_offsets, sums, taken):
-    points = taken[0].shape[1] - EXTRA
+def finish(members, all_points, lag_offsets, sums, folded):
+    points = folded[0].shape[1] - EXTRA
     lags = lag_offsets.shape[0]
     return pl.pallas_call(
-        lambda *refs: finish_kernel(members, total_days, all_points, *refs),
-        in_specs=[pl.BlockSpec(memory_space=pltpu.SMEM)] + [vmem()] * (2 * SIDE + 1),
+        lambda *refs: finish_kernel(members, all_points, *refs),
+        in_specs=[pl.BlockSpec(memory_space=pltpu.SMEM)] + [vmem()] * 3,
         scratch_shapes=[pltpu.VMEM((TILE, points), F32)],
         out_shape=jax.ShapeDtypeStruct((lags, 2, points), F32),
         compiler_params=pltpu.CompilerParams(vmem_limit_bytes=MERGE_VMEM),
         name="finish",
-    )(lag_offsets, sums, *taken)
+    )(lag_offsets, sums, *folded)
 
 
 def swap(value, axis, mask):
     return lax.ppermute(value, axis, [(i, i ^ mask) for i in range(lax.axis_size(axis))])
-
-
-def map_sums(sums):
-    types, space = sums.shape[0], lax.axis_size("space")
-    chips = space // 2
-    sums = jnp.broadcast_to(sums[:, None], (types, chips, sums.shape[1]))
-    groups = [[2 * i + core for i in range(types * chips)] for core in range(2)]
-    return lax.all_to_all(
-        sums.reshape(types * chips, -1), ("tm", "space"), 0, 0, axis_index_groups=groups, tiled=True
-    )
 
 
 def shards(fields, calendar_day, events, lag_offsets):
@@ -350,17 +369,17 @@
     total_days = fields.shape[0] * lax.axis_size("tm")
     all_points = fields.shape[2] * lax.axis_size("space")
     *sent, sums = products(me, events, calendar_day, fields)
-    sent, sums = lax.optimization_barrier((sent, sums + swap(sums, "space", 1)))
     mine = [[sent[0]] + [None] * 3, [sent[SIDE]] + [None] * 3]
-    for r in (2, 1, 3):
-        mine[0][r] = swap(sent[r], "tm", SIDE * r)
-        mine[1][r] = swap(sent[SIDE + r], "tm", r)
-    sums = map_sums(sums)
-    taken = []
+    for r in (3, 1, 2):
+        mine[0][r] = swap(sent[r], "tm", near(r))
+        mine[1][r] = swap(sent[SIDE + r], "tm", far(r))
+    sums = lax.all_to_all(sums, ("tm", "space"), 0, 0, tiled=True)
+    folded = []
     for v in range(2):
         parts = merge(mine[v], members, total_days)
-        taken += [parts[0]] + [swap(parts[r], "tm", r if v == 0 else SIDE * r) for r in (1, 2, 3)]
-    return finish(members, total_days, all_points, lag_offsets, sums, taken)[None]
+        got = [swap(parts[r], "tm", far(r) if v == 0 else near(r)) for r in (1, 2, 3)]
+        folded.append(fold(v, [parts[0]] + got, members, total_days))
+    return finish(members, all_points, lag_offsets, sums, folded)[None]
 
 
 def solution(mesh):

time: 77.9 us -> 64.2 us (0.82)
  the two profiles are of different devices: /device:TPU:8 before, /device:TPU:1 now
where the time goes in v1:
time: 64.2 us; the launch traced here: 63.4 us
  starting transfers between devices  38.7 us (60%)
  Pallas kernels  16.8 us (26%)
  waiting for transfers between devices  7.22 us (11%)
  local copies, waits for them, and re-layouts  0.66 us (1%)
    ppermute x12, starting transfers between devices, swap(): lax.ppermute(value, axis, [(i, i ^ mask) for i in range(lax.axis_size(axi...  25.1 us
    all_to_all x1, starting transfers between devices, shards(): sums = lax.all_to_all(sums, ('tm', 'space'), 0, 0, tiled=True)  13.6 us
    pallas_call x1, Pallas kernels, products(): pl.pallas_call(lambda *refs: products_kernel(local_days * tm, *refs), in_...  10.9 us
    ppermute x12, waiting for transfers between devices, swap(): lax.ppermute(value, axis, [(i, i ^ mask) for i in range(lax.axis_size(axi...  7.22 us
    pallas_call x2, Pallas kernels, fold(): pl.pallas_call(lambda *refs: fold_kernel(v, members, total_days, *refs),...  2.29 us
    pallas_call x2, Pallas kernels, merge(): pl.pallas_call(lambda *refs: merge_kernel(members, total_days, *refs), in...  2.09 us
    pallas_call x1, Pallas kernels, finish(): pl.pallas_call(lambda *refs: finish_kernel(members, all_points, *refs), i...  1.46 us
  transfers between devices with their start and end apart: 13, of which 3 were waited for; matrix products, arithmetic and copies ran while one was open for 0% of the time, Pallas kernels for 7%

profile of v1, /device:TPU:1, one launch (start us, length us, event | category | flops | bytes accessed | tf_op | source)
XLA Modules:
  0.0 63.4 jit_solution(9382634616569667900)
XLA Ops:
  0.0 0.0 copy-start
  0.0 10.9 %products.1 = (f32[80,2176]{1,0:T(8,128)S(1)}, s16[80,2176]{1,0:T(8,128)(2,1)S(1)}, s16[80,2176]{1,0:T(8,128)(2,1)S(1)}, s16[80,2176]{1,0:T(8,128)(2,1)S(1)}, f3...) custom-call(s32[1]{0:T(128)} %bitcast.refs_0_, ...), custom_call_target="tpu_custom_call" | custom-call | tf_op jit(solution)/shard_map/products/pallas_call | solution.py:247
  10.9 2.1 %collective-permute-start = (s16[80,2176]{1,0:T(8,128)(2,1)S(1)}, s16[80,2176]{1,0:T(8,128)(2,1)S(1)}, u32[]{:S(2)}, u32[]{:S(2)}) collective-permute-start(s16[80,2176]{1,0:T(8,128)(2,1)S(1)} %get-tuple-element.24), channel_id=1, source_target_pairs={{0,64},{16,80},{32,96},{48,112},{64,0},{80,16},{96,32},{112,48},{1... | collective-permute-start | bytes 1044488 | tf_op jit(solution)/shard_map/ppermute | solution.py:363
  13.0 1.3 %collective-permute-start.1 = (s16[80,2176]{1,0:T(8,128)(2,1)S(1)}, s16[80,2176]{1,0:T(8,128)(2,1)S(1)}, u32[]{:S(2)}, u32[]{:S(2)}) collective-permute-start(s16[80,2176]{1,0:T(8,128)(2,1)S(1)} %get-tuple-element.25), channel_id=1, source_target_pairs={{0,16},{16,0},{32,48},{48,32},{64,80},{80,64},{96,112},{112,96},{1... | collective-permute-start | bytes 1044488 | tf_op jit(solution)/shard_map/ppermute | solution.py:363
  14.3 0.0 collective-permute-start.2
  14.3 2.6 %collective-permute-start.6 = (s16[80,2176]{1,0:T(8,128)(2,1)S(1)}, s16[80,2176]{1,0:T(8,128)(2,1)S(1)}, u32[]{:S(2)}, u32[]{:S(2)}) collective-permute-start(s16[80,2176]{1,0:T(8,128)(2,1)S(1)} %get-tuple-element.32), channel_id=1, source_target_pairs={{0,192},{16,208},{32,224},{48,240},{64,128},{80,144},{96,160},{112... | collective-permute-start | bytes 1044488 | tf_op jit(solution)/shard_map/ppermute | solution.py:363
  17.0 2.7 %collective-permute-start.7 = (s16[80,2176]{1,0:T(8,128)(2,1)S(1)}, s16[80,2176]{1,0:T(8,128)(2,1)S(1)}, u32[]{:S(2)}, u32[]{:S(2)}) collective-permute-start(s16[80,2176]{1,0:T(8,128)(2,1)S(1)} %get-tuple-element.33), channel_id=1, source_target_pairs={{0,48},{16,32},{32,16},{48,0},{64,112},{80,96},{96,80},{112,64},{1... | collective-permute-start | bytes 1044488 | tf_op jit(solution)/shard_map/ppermute | solution.py:363
  19.7 0.0 collective-permute-done.refs_1_
  19.7 6.1 %collective-permute-start.8 = (s16[80,2176]{1,0:T(8,128)(2,1)S(1)}, s16[80,2176]{1,0:T(8,128)(2,1)S(1)}, u32[]{:S(2)}, u32[]{:S(2)}) collective-permute-start(s16[80,2176]{1,0:T(8,128)(2,1)S(1)} %get-tuple-element.34), channel_id=1, source_target_pairs={{0,240},{16,224},{32,208},{48,192},{64,176},{80,160},{96,144},{112... | collective-permute-start | bytes 1044488 | tf_op jit(solution)/shard_map/ppermute | solution.py:363
  25.8 0.0 collective-permute-done.1.refs_2_
  25.8 3.6 %collective-permute-done.2.refs_3_ = s16[80,2176]{1,0:T(8,128)(2,1)S(1)} collective-permute-done((s16[80,2176]{1,0:T(8,128)(2,1)S(1)}, s16[80,2176]{1,0:T(8,128)(2,1)S(1)}, u32[]{:S(2)}, u32[]{:S(2)}) %collective-permute-start.2) | collective-permute-done | bytes 348192 | tf_op jit(solution)/shard_map/ppermute | solution.py:363
  29.4 1.4 %merge.2 = (f32[32,2176]{1,0:T(8,128)S(1)}, s16[32,2176]{1,0:T(8,128)(2,1)}, s16[32,2176]{1,0:T(8,128)(2,1)S(1)}, s16[32,2176]{1,0:T(8,128)(2,1)S(1)}) custom-call(f32[80,2176]{1,0:T(8,128)S(1)} %get-tuple-element.23.refs_0_, s16[80,2176]{1,0:T(8,128)(2,1)S(1)} %collective-permute-done.refs_1_, s16[80,2176]{1,0:T(8,128)(2,1)S(1)} %collective-permute-done.1.refs_2_, ...), custom_call_target="tpu_custom_call" | custom-call | tf_op jit(solution)/shard_map/merge/pallas_call | solution.py:297
  30.8 0.0 copy-start.1
  30.8 0.7 %copy-done.1 = s16[32,2176]{1,0:T(8,128)(2,1)} copy-done((s16[32,2176]{1,0:T(8,128)(2,1)}, s16[32,2176]{1,0:T(8,128)(2,1)S(1)}, u32[]{:S(2)}) %copy-start.1) | copy-done | bytes 139288
  31.4 2.4 %collective-permute-start.3 = (s16[32,2176]{1,0:T(8,128)(2,1)}, s16[32,2176]{1,0:T(8,128)(2,1)S(1)}, u32[]{:S(2)}, u32[]{:S(2)}) collective-permute-start(s16[32,2176]{1,0:T(8,128)(2,1)} %get-tuple-element.28), channel_id=1, source_target_pairs={{0,192},{16,208},{32,224},{48,240},{64,128},{80,144},{96,160},{112... | collective-permute-start | bytes 417800 | tf_op jit(solution)/shard_map/ppermute | solution.py:363
  33.8 13.6 %all-to-all-start = ((f32[256,1,128]{2,1,0:T(1,128)}), f32[256,1,128]{2,1,0:T(1,128)S(1)}, u32[]{:S(2)}, u32[]{:S(2)}) async-start(f32[256,1,128]{2,1,0:T(1,128)} %bitcast.3), calls=%async_computation | async-start | bytes 262144 | tf_op jit(solution)/shard_map/all_to_all | solution.py:376
  47.5 2.7 %collective-permute-start.4 = (s16[32,2176]{1,0:T(8,128)(2,1)}, s16[32,2176]{1,0:T(8,128)(2,1)S(1)}, u32[]{:S(2)}, u32[]{:S(2)}) collective-permute-start(s16[32,2176]{1,0:T(8,128)(2,1)} %copy-done.1), channel_id=1, source_target_pairs={{0,48},{16,32},{32,16},{48,0},{64,112},{80,96},{96,80},{112,64},{1... | collective-permute-start | bytes 417800 | tf_op jit(solution)/shard_map/ppermute | solution.py:363
  50.2 0.0 collective-permute-done.6.refs_1_
  50.2 2.3 %collective-permute-start.5 = (s16[32,2176]{1,0:T(8,128)(2,1)S(1)}, s16[32,2176]{1,0:T(8,128)(2,1)S(1)}, u32[]{:S(2)}, u32[]{:S(2)}) collective-permute-start(s16[32,2176]{1,0:T(8,128)(2,1)S(1)} %get-tuple-element.30), channel_id=1, source_target_pairs={{0,240},{16,224},{32,208},{48,192},{64,176},{80,160},{96,144},{112... | collective-permute-start | bytes 417800 | tf_op jit(solution)/shard_map/ppermute | solution.py:363
  52.5 0.0 collective-permute-done.7.refs_2_
  52.5 0.0 collective-permute-done.8.refs_3_
  52.5 0.7 %merge.3 = (f32[32,2176]{1,0:T(8,128)S(1)}, s16[32,2176]{1,0:T(8,128)(2,1)S(1)}, s16[32,2176]{1,0:T(8,128)(2,1)S(1)}, s16[32,2176]{1,0:T(8,128)(2,1)S(1)}) custom-call(f32[80,2176]{1,0:T(8,128)S(1)} %get-tuple-element.31.refs_0_, s16[80,2176]{1,0:T(8,128)(2,1)S(1)} %collective-permute-done.6.refs_1_, s16[80,2176]{1,0:T(8,128)(2,1)S(1)} %collective-permute-done.7.refs_2_, ...), custom_call_target="tpu_custom_call" | custom-call | tf_op jit(solution)/shard_map/merge/pallas_call | solution.py:297
  53.3 0.1 collective-permute-start.9
  53.4 0.1 collective-permute-start.10
  53.5 0.0 collective-permute-done.3.refs_1_
  53.5 2.5 %collective-permute-start.11 = (s16[32,2176]{1,0:T(8,128)(2,1)S(1)}, s16[32,2176]{1,0:T(8,128)(2,1)S(1)}, u32[]{:S(2)}, u32[]{:S(2)}) collective-permute-start(s16[32,2176]{1,0:T(8,128)(2,1)S(1)} %get-tuple-element.38), channel_id=1, source_target_pairs={{0,80},{16,64},{32,112},{48,96},{64,16},{80,0},{96,48},{112,32},{1... | collective-permute-start | bytes 417800 | tf_op jit(solution)/shard_map/ppermute | solution.py:363
  56.0 0.0 collective-permute-done.4.refs_2_
  56.0 3.0 %collective-permute-done.5.refs_3_ = s16[32,2176]{1,0:T(8,128)(2,1)S(1)} collective-permute-done((s16[32,2176]{1,0:T(8,128)(2,1)S(1)}, s16[32,2176]{1,0:T(8,128)(2,1)S(1)}, u32[]{:S(2)}, u32[]{:S(2)}) %collective-permute-start.5) | collective-permute-done | bytes 139296 | tf_op jit(solution)/shard_map/ppermute | solution.py:363
  59.0 1.1 %fold.2.refs_2_ = f32[16,2176]{1,0:T(8,128)S(1)} custom-call(f32[32,2176]{1,0:T(8,128)S(1)} %get-tuple-element.27.refs_0_, s16[32,2176]{1,0:T(8,128)(2,1)S(1)} %collective-permute-done.3.refs_1_, s16[32,2176]{1,0:T(8,128)(2,1)S(1)} %collective-permute-done.4.refs_2_, s16[32,2176]{1,0:T(8,128)(2,1)S(1)} %collective-permute-done.5.refs_3_), custom_call_target="tpu_custom_call" | custom-call | tf_op jit(solution)/shard_map/fold/pallas_call | solution.py:324
  60.2 0.0 collective-permute-done.9.refs_1_
  60.2 0.0 collective-permute-done.10.refs_2_
  60.2 0.6 collective-permute-done.11.refs_3_
  60.8 1.1 %fold.3.refs_3_ = f32[16,2176]{1,0:T(8,128)S(1)} custom-call(f32[32,2176]{1,0:T(8,128)S(1)} %get-tuple-element.35.refs_0_, s16[32,2176]{1,0:T(8,128)(2,1)S(1)} %collective-permute-done.9.refs_1_, s16[32,2176]{1,0:T(8,128)(2,1)S(1)} %collective-permute-done.10.refs_2_, s16[32,2176]{1,0:T(8,128)(2,1)S(1)} %collective-permute-done.11.refs_3_), custom_call_target="tpu_custom_call" | custom-call | tf_op jit(solution)/shard_map/fold/pallas_call | solution.py:324
  61.9 0.0 all-to-all-done
  61.9 0.0 copy-done
  62.0 1.5 %finish.1 = f32[16,2,2048]{2,1,0:T(2,128)} custom-call(s32[16]{0:T(128)S(1)} %copy-done, f32[256,128]{1,0:T(8,128)S(1)} %bitcast.7, f32[16,2176]{1,0:T(8,128)S(1)} %fold.2.refs_2_, f32[16,2176]{1,0:T(8,128)S(1)} %fold.3.refs_3_), custom_call_target="tpu_custom_call" | custom-call | tf_op jit(solution)/shard_map/finish/pallas_call | solution.py:352
Async XLA Ops:
  0.0 61.9 %copy-start = (s32[16]{0:T(128)S(1)}, s32[16]{0:T(128)}, u32[]{:S(2)}) copy-start(s32[16]{0:T(128)} %refs_0_.1) | copy-start | bytes 196
  10.9 8.8 %collective-permute-start = (s16[80,2176]{1,0:T(8,128)(2,1)S(1)}, s16[80,2176]{1,0:T(8,128)(2,1)S(1)}, u32[]{:S(2)}, u32[]{:S(2)}) collective-permute-start(s16[80,2176]{1,0:T(8,128)(2,1)S(1)} %get-tuple-element.24), channel_id=1, source_target_pairs={{0,64},{16,80},{32,96},{48,112},{64,0},{80,16},{96,32},{112,48},{1... | collective-permute-start | bytes 1044488 | tf_op jit(solution)/shard_map/ppermute | solution.py:363
  13.0 12.8 %collective-permute-start.1 = (s16[80,2176]{1,0:T(8,128)(2,1)S(1)}, s16[80,2176]{1,0:T(8,128)(2,1)S(1)}, u32[]{:S(2)}, u32[]{:S(2)}) collective-permute-start(s16[80,2176]{1,0:T(8,128)(2,1)S(1)} %get-tuple-element.25), channel_id=1, source_target_pairs={{0,16},{16,0},{32,48},{48,32},{64,80},{80,64},{96,112},{112,96},{1... | collective-permute-start | bytes 1044488 | tf_op jit(solution)/shard_map/ppermute | solution.py:363
  14.3 15.1 %collective-permute-start.2 = (s16[80,2176]{1,0:T(8,128)(2,1)S(1)}, s16[80,2176]{1,0:T(8,128)(2,1)S(1)}, u32[]{:S(2)}, u32[]{:S(2)}) collective-permute-start(s16[80,2176]{1,0:T(8,128)(2,1)S(1)} %get-tuple-element.26), channel_id=1, source_target_pairs={{0,80},{16,64},{32,112},{48,96},{64,16},{80,0},{96,48},{112,32},{1... | collective-permute-start | bytes 1044488 | tf_op jit(solution)/shard_map/ppermute | solution.py:363
  14.3 35.8 %collective-permute-start.6 = (s16[80,2176]{1,0:T(8,128)(2,1)S(1)}, s16[80,2176]{1,0:T(8,128)(2,1)S(1)}, u32[]{:S(2)}, u32[]{:S(2)}) collective-permute-start(s16[80,2176]{1,0:T(8,128)(2,1)S(1)} %get-tuple-element.32), channel_id=1, source_target_pairs={{0,192},{16,208},{32,224},{48,240},{64,128},{80,144},{96,160},{112... | collective-permute-start | bytes 1044488 | tf_op jit(solution)/shard_map/ppermute | solution.py:363
  17.0 35.6 %collective-permute-start.7 = (s16[80,2176]{1,0:T(8,128)(2,1)S(1)}, s16[80,2176]{1,0:T(8,128)(2,1)S(1)}, u32[]{:S(2)}, u32[]{:S(2)}) collective-permute-start(s16[80,2176]{1,0:T(8,128)(2,1)S(1)} %get-tuple-element.33), channel_id=1, source_target_pairs={{0,48},{16,32},{32,16},{48,0},{64,112},{80,96},{96,80},{112,64},{1... | collective-permute-start | bytes 1044488 | tf_op jit(solution)/shard_map/ppermute | solution.py:363
  19.7 32.8 %collective-permute-start.8 = (s16[80,2176]{1,0:T(8,128)(2,1)S(1)}, s16[80,2176]{1,0:T(8,128)(2,1)S(1)}, u32[]{:S(2)}, u32[]{:S(2)}) collective-permute-start(s16[80,2176]{1,0:T(8,128)(2,1)S(1)} %get-tuple-element.34), channel_id=1, source_target_pairs={{0,240},{16,224},{32,208},{48,192},{64,176},{80,160},{96,144},{112... | collective-permute-start | bytes 1044488 | tf_op jit(solution)/shard_map/ppermute | solution.py:363
  30.8 0.7 %copy-start.1 = (s16[32,2176]{1,0:T(8,128)(2,1)}, s16[32,2176]{1,0:T(8,128)(2,1)S(1)}, u32[]{:S(2)}) copy-start(s16[32,2176]{1,0:T(8,128)(2,1)S(1)} %get-tuple-element.29) | copy-start | bytes 417796
  31.4 22.0 %collective-permute-start.3 = (s16[32,2176]{1,0:T(8,128)(2,1)}, s16[32,2176]{1,0:T(8,128)(2,1)S(1)}, u32[]{:S(2)}, u32[]{:S(2)}) collective-permute-start(s16[32,2176]{1,0:T(8,128)(2,1)} %get-tuple-element.28), channel_id=1, source_target_pairs={{0,192},{16,208},{32,224},{48,240},{64,128},{80,144},{96,160},{112... | collective-permute-start | bytes 417800 | tf_op jit(solution)/shard_map/ppermute | solution.py:363
  33.8 28.1 %all-to-all-start = ((f32[256,1,128]{2,1,0:T(1,128)}), f32[256,1,128]{2,1,0:T(1,128)S(1)}, u32[]{:S(2)}, u32[]{:S(2)}) async-start(f32[256,1,128]{2,1,0:T(1,128)} %bitcast.3), calls=%async_computation | async-start | bytes 262144 | tf_op jit(solution)/shard_map/all_to_all | solution.py:376
  47.5 8.5 %collective-permute-start.4 = (s16[32,2176]{1,0:T(8,128)(2,1)}, s16[32,2176]{1,0:T(8,128)(2,1)S(1)}, u32[]{:S(2)}, u32[]{:S(2)}) collective-permute-start(s16[32,2176]{1,0:T(8,128)(2,1)} %copy-done.1), channel_id=1, source_target_pairs={{0,48},{16,32},{32,16},{48,0},{64,112},{80,96},{96,80},{112,64},{1... | collective-permute-start | bytes 417800 | tf_op jit(solution)/shard_map/ppermute | solution.py:363
  50.2 8.8 %collective-permute-start.5 = (s16[32,2176]{1,0:T(8,128)(2,1)S(1)}, s16[32,2176]{1,0:T(8,128)(2,1)S(1)}, u32[]{:S(2)}, u32[]{:S(2)}) collective-permute-start(s16[32,2176]{1,0:T(8,128)(2,1)S(1)} %get-tuple-element.30), channel_id=1, source_target_pairs={{0,240},{16,224},{32,208},{48,192},{64,176},{80,160},{96,144},{112... | collective-permute-start | bytes 417800 | tf_op jit(solution)/shard_map/ppermute | solution.py:363
  53.3 6.9 %collective-permute-start.9 = (s16[32,2176]{1,0:T(8,128)(2,1)S(1)}, s16[32,2176]{1,0:T(8,128)(2,1)S(1)}, u32[]{:S(2)}, u32[]{:S(2)}) collective-permute-start(s16[32,2176]{1,0:T(8,128)(2,1)S(1)} %get-tuple-element.36), channel_id=1, source_target_pairs={{0,64},{16,80},{32,96},{48,112},{64,0},{80,16},{96,32},{112,48},{1... | collective-permute-start | bytes 417800 | tf_op jit(solution)/shard_map/ppermute | solution.py:363
  53.4 6.8 %collective-permute-start.10 = (s16[32,2176]{1,0:T(8,128)(2,1)S(1)}, s16[32,2176]{1,0:T(8,128)(2,1)S(1)}, u32[]{:S(2)}, u32[]{:S(2)}) collective-permute-start(s16[32,2176]{1,0:T(8,128)(2,1)S(1)} %get-tuple-element.37), channel_id=1, source_target_pairs={{0,16},{16,0},{32,48},{48,32},{64,80},{80,64},{96,112},{112,96},{1... | collective-permute-start | bytes 417800 | tf_op jit(solution)/shard_map/ppermute | solution.py:363
  53.5 7.3 %collective-permute-start.11 = (s16[32,2176]{1,0:T(8,128)(2,1)S(1)}, s16[32,2176]{1,0:T(8,128)(2,1)S(1)}, u32[]{:S(2)}, u32[]{:S(2)}) collective-permute-start(s16[32,2176]{1,0:T(8,128)(2,1)S(1)} %get-tuple-element.38), channel_id=1, source_target_pairs={{0,80},{16,64},{32,112},{48,96},{64,16},{80,0},{96,48},{112,32},{1... | collective-permute-start | bytes 417800 | tf_op jit(solution)/shard_map/ppermute | solution.py:363

commit v2 on v1

--- a/solution.py
+++ b/solution.py
@@ -166,9 +166,12 @@
     rows = SIDE * group
     half = rows + TILE
     chunks = [slice(c, c + CHUNK) for c in range(0, points, CHUNK)]
+    block = fields_ref.shape[0] // len(chunks)
     copies = [
-        pltpu.make_async_copy(fields_ref.at[:, :, c], record_ref.at[:, :, c], arrived.at[i])
-        for i, c in enumerate(chunks)
+        pltpu.make_async_copy(
+            fields_ref.at[pl.ds(block * i, block)], record_ref.at[pl.ds(block * i, block)], arrived.at[i]
+        )
+        for i in range(len(chunks))
     ]
     small = [
         pltpu.make_async_copy(events_ref, own_events, arrived.at[len(chunks)]),
@@ -186,8 +189,9 @@
             left, jnp.concatenate([left[rows:, :], pad], axis=0)
         )
     record = record_ref.reshape(2 * record_ref.shape[0], points)
-    for copy, c in zip(copies, chunks):
+    for copy in copies:
         copy.wait()
+    for c in chunks:
         all_ref[:, c] = dot(left_ref[...], record[:, c])
     for r in (2, 1, 3, 0):
         for v in range(2):
@@ -282,12 +286,14 @@
 
 
 def merge_kernel(members, total_days, *refs):
-    taken, outs = refs[:SIDE], refs[SIDE:]
-    main, aux = added(taken, members, total_days)
-    for r in (2, 1, 3):
-        encode(outs[r], main[TILE * r : TILE * (r + 1)], aux, members, total_days)
-    outs[0][:TILE, :] = main[:TILE]
-    outs[0][TILE:, :] = aux
+    for v in range(2):
+        taken = refs[SIDE * v : SIDE * (v + 1)]
+        outs = refs[SIDE * (v + 2) : SIDE * (v + 3)]
+        main, aux = added(taken, members, total_days)
+        for r in (3, 1, 2):
+            encode(outs[r], main[TILE * r : TILE * (r + 1)], aux, members, total_days)
+        outs[0][:TILE, :] = main[:TILE]
+        outs[0][TILE:, :] = aux
 
 
 def merge(taken, members, total_days):
@@ -296,9 +302,9 @@
     message = jax.ShapeDtypeStruct((2 * TILE, columns), jnp.int16)
     return pl.pallas_call(
         lambda *refs: merge_kernel(members, total_days, *refs),
-        in_specs=[vmem()] * SIDE,
-        out_specs=[vmem()] * SIDE,
-        out_shape=[kept] + [message] * (SIDE - 1),
+        in_specs=[vmem()] * (2 * SIDE),
+        out_specs=[vmem()] * (2 * SIDE),
+        out_shape=([kept] + [message] * (SIDE - 1)) * 2,
         compiler_params=pltpu.CompilerParams(vmem_limit_bytes=MERGE_VMEM),
         name="merge",
     )(*taken)
@@ -374,11 +380,12 @@
         mine[0][r] = swap(sent[r], "tm", near(r))
         mine[1][r] = swap(sent[SIDE + r], "tm", far(r))
     sums = lax.all_to_all(sums, ("tm", "space"), 0, 0, tiled=True)
-    folded = []
-    for v in range(2):
-        parts = merge(mine[v], members, total_days)
-        got = [swap(parts[r], "tm", far(r) if v == 0 else near(r)) for r in (1, 2, 3)]
-        folded.append(fold(v, [parts[0]] + got, members, total_days))
+    parts = merge(mine[0] + mine[1], members, total_days)
+    got = [[parts[0]] + [None] * 3, [parts[SIDE]] + [None] * 3]
+    for r in (3, 1, 2):
+        got[0][r] = swap(parts[r], "tm", far(r))
+        got[1][r] = swap(parts[SIDE + r], "tm", near(r))
+    folded = [fold(v, got[v], members, total_days) for v in range(2)]
     return finish(members, all_points, lag_offsets, sums, folded)[None]
 
 

time: 64.2 us -> 67.6 us (1.053)
  waiting for transfers between devices: 7.22 us -> 10.5 us
  starting transfers between devices: 38.7 us -> 40.6 us
  Pallas kernels: 16.8 us -> 15.7 us
    ppermute x12, waiting for transfers between devices: 7.22 us -> 10.5 us  [swap(): lax.ppermute(value, axis, [(i, i ^ mask) for i in range(lax.axis_size(axi...]
    ppermute x12, starting transfers between devices: 25.1 us -> 26.8 us  [swap(): lax.ppermute(value, axis, [(i, i ^ mask) for i in range(lax.axis_size(axi...]
    pallas_call x1, Pallas kernels: 10.9 us -> 10.2 us  [products(): pl.pallas_call(lambda *refs: products_kernel(local_days * tm, *refs), in_...]
    pallas_call x2 -> x1, Pallas kernels: 2.09 us -> 1.72 us  [merge(): pl.pallas_call(lambda *refs: merge_kernel(members, total_days, *refs), in...]
  transfers between devices with their start and end apart: 13 -> 13, of which waited for: 3 -> 5; matrix products, arithmetic and copies ran while one was open for 0% -> 0% of each run, Pallas kernels for 7% -> 3%
where the time goes in v2:
time: 67.6 us; the launch traced here: 66.9 us
  starting transfers between devices  40.6 us (60%)
  Pallas kernels  15.7 us (23%)
  waiting for transfers between devices  10.5 us (16%)
    ppermute x12, starting transfers between devices, swap(): lax.ppermute(value, axis, [(i, i ^ mask) for i in range(lax.axis_size(axi...  26.8 us
    all_to_all x1, starting transfers between devices, shards(): sums = lax.all_to_all(sums, ('tm', 'space'), 0, 0, tiled=True)  13.8 us
    ppermute x12, waiting for transfers between devices, swap(): lax.ppermute(value, axis, [(i, i ^ mask) for i in range(lax.axis_size(axi...  10.5 us
    pallas_call x1, Pallas kernels, products(): pl.pallas_call(lambda *refs: products_kernel(local_days * tm, *refs), in_...  10.2 us
    pallas_call x2, Pallas kernels, fold(): pl.pallas_call(lambda *refs: fold_kernel(v, members, total_days, *refs),...  2.28 us
    pallas_call x1, Pallas kernels, merge(): pl.pallas_call(lambda *refs: merge_kernel(members, total_days, *refs), in...  1.72 us
    pallas_call x1, Pallas kernels, finish(): pl.pallas_call(lambda *refs: finish_kernel(members, all_points, *refs), i...  1.46 us
  transfers between devices with their start and end apart: 13, of which 5 were waited for; matrix products, arithmetic and copies ran while one was open for 0% of the time, Pallas kernels for 3%

profile of v2, /device:TPU:1, one launch (start us, length us, event | category | flops | bytes accessed | tf_op | source)
XLA Modules:
  0.0 66.9 jit_solution(2163427191132476241)
XLA Ops:
  0.0 0.0 copy-start
  0.0 10.2 %products.1 = (f32[80,2176]{1,0:T(8,128)S(1)}, s16[80,2176]{1,0:T(8,128)(2,1)S(1)}, s16[80,2176]{1,0:T(8,128)(2,1)S(1)}, s16[80,2176]{1,0:T(8,128)(2,1)S(1)}, f3...) custom-call(s32[1]{0:T(128)} %bitcast.refs_0_, ...), custom_call_target="tpu_custom_call" | custom-call | tf_op jit(solution)/shard_map/products/pallas_call | solution.py:251
  10.2 2.1 %collective-permute-start = (s16[80,2176]{1,0:T(8,128)(2,1)S(1)}, s16[80,2176]{1,0:T(8,128)(2,1)S(1)}, u32[]{:S(2)}, u32[]{:S(2)}) collective-permute-start(s16[80,2176]{1,0:T(8,128)(2,1)S(1)} %get-tuple-element.24), channel_id=1, source_target_pairs={{0,64},{16,80},{32,96},{48,112},{64,0},{80,16},{96,32},{112,48},{1... | collective-permute-start | bytes 1044488 | tf_op jit(solution)/shard_map/ppermute | solution.py:369
  12.3 1.3 %collective-permute-start.1 = (s16[80,2176]{1,0:T(8,128)(2,1)S(1)}, s16[80,2176]{1,0:T(8,128)(2,1)S(1)}, u32[]{:S(2)}, u32[]{:S(2)}) collective-permute-start(s16[80,2176]{1,0:T(8,128)(2,1)S(1)} %get-tuple-element.25), channel_id=1, source_target_pairs={{0,16},{16,0},{32,48},{48,32},{64,80},{80,64},{96,112},{112,96},{1... | collective-permute-start | bytes 1044488 | tf_op jit(solution)/shard_map/ppermute | solution.py:369
  13.6 0.0 collective-permute-start.2
  13.6 2.6 %collective-permute-start.3 = (s16[80,2176]{1,0:T(8,128)(2,1)S(1)}, s16[80,2176]{1,0:T(8,128)(2,1)S(1)}, u32[]{:S(2)}, u32[]{:S(2)}) collective-permute-start(s16[80,2176]{1,0:T(8,128)(2,1)S(1)} %get-tuple-element.28), channel_id=1, source_target_pairs={{0,192},{16,208},{32,224},{48,240},{64,128},{80,144},{96,160},{112... | collective-permute-start | bytes 1044488 | tf_op jit(solution)/shard_map/ppermute | solution.py:369
  16.3 2.7 %collective-permute-start.4 = (s16[80,2176]{1,0:T(8,128)(2,1)S(1)}, s16[80,2176]{1,0:T(8,128)(2,1)S(1)}, u32[]{:S(2)}, u32[]{:S(2)}) collective-permute-start(s16[80,2176]{1,0:T(8,128)(2,1)S(1)} %get-tuple-element.29), channel_id=1, source_target_pairs={{0,48},{16,32},{32,16},{48,0},{64,112},{80,96},{96,80},{112,64},{1... | collective-permute-start | bytes 1044488 | tf_op jit(solution)/shard_map/ppermute | solution.py:369
  19.0 0.0 collective-permute-done.refs_1_
  19.0 6.1 %collective-permute-start.5 = (s16[80,2176]{1,0:T(8,128)(2,1)S(1)}, s16[80,2176]{1,0:T(8,128)(2,1)S(1)}, u32[]{:S(2)}, u32[]{:S(2)}) collective-permute-start(s16[80,2176]{1,0:T(8,128)(2,1)S(1)} %get-tuple-element.30), channel_id=1, source_target_pairs={{0,240},{16,224},{32,208},{48,192},{64,176},{80,160},{96,144},{112... | collective-permute-start | bytes 1044488 | tf_op jit(solution)/shard_map/ppermute | solution.py:369
  25.1 0.0 collective-permute-done.1.refs_2_
  25.1 3.6 %collective-permute-done.2.refs_3_ = s16[80,2176]{1,0:T(8,128)(2,1)S(1)} collective-permute-done((s16[80,2176]{1,0:T(8,128)(2,1)S(1)}, s16[80,2176]{1,0:T(8,128)(2,1)S(1)}, u32[]{:S(2)}, u32[]{:S(2)}) %collective-permute-start.2) | collective-permute-done | bytes 348192 | tf_op jit(solution)/shard_map/ppermute | solution.py:369
  28.7 0.0 collective-permute-done.3.refs_5_
  28.7 0.0 collective-permute-done.4.refs_6_
  28.7 3.0 %collective-permute-done.5.refs_7_ = s16[80,2176]{1,0:T(8,128)(2,1)S(1)} collective-permute-done((s16[80,2176]{1,0:T(8,128)(2,1)S(1)}, s16[80,2176]{1,0:T(8,128)(2,1)S(1)}, u32[]{:S(2)}, u32[]{:S(2)}) %collective-permute-start.5) | collective-permute-done | bytes 348192 | tf_op jit(solution)/shard_map/ppermute | solution.py:369
  31.7 1.7 %merge.1 = (f32[32,2176]{1,0:T(8,128)S(1)}, s16[32,2176]{1,0:T(8,128)(2,1)S(1)}, s16[32,2176]{1,0:T(8,128)(2,1)S(1)}, s16[32,2176]{1,0:T(8,128)(2,1)S(1)}, f32[3...) custom-call(f32[80,2176]{1,0:T(8,128)S(1)} %get-tuple-element.23.ref, ...), custom_call_target="tpu_custom_call" | custom-call | tf_op jit(solution)/shard_map/merge/pallas_call | solution.py:303
  33.4 4.3 %collective-permute-start.6 = (s16[32,2176]{1,0:T(8,128)(2,1)S(1)}, s16[32,2176]{1,0:T(8,128)(2,1)S(1)}, u32[]{:S(2)}, u32[]{:S(2)}) collective-permute-start(s16[32,2176]{1,0:T(8,128)(2,1)S(1)} %get-tuple-element.32), channel_id=1, source_target_pairs={{0,192},{16,208},{32,224},{48,240},{64,128},{80,144},{96,160},{112... | collective-permute-start | bytes 417800 | tf_op jit(solution)/shard_map/ppermute | solution.py:369
  37.7 13.8 %all-to-all-start = ((f32[256,1,128]{2,1,0:T(1,128)}), f32[256,1,128]{2,1,0:T(1,128)S(1)}, u32[]{:S(2)}, u32[]{:S(2)}) async-start(f32[256,1,128]{2,1,0:T(1,128)} %bitcast.3), calls=%async_computation | async-start | bytes 262144 | tf_op jit(solution)/shard_map/all_to_all | solution.py:382
  51.5 2.7 %collective-permute-start.7 = (s16[32,2176]{1,0:T(8,128)(2,1)S(1)}, s16[32,2176]{1,0:T(8,128)(2,1)S(1)}, u32[]{:S(2)}, u32[]{:S(2)}) collective-permute-start(s16[32,2176]{1,0:T(8,128)(2,1)S(1)} %get-tuple-element.33), channel_id=1, source_target_pairs={{0,48},{16,32},{32,16},{48,0},{64,112},{80,96},{96,80},{112,64},{1... | collective-permute-start | bytes 417800 | tf_op jit(solution)/shard_map/ppermute | solution.py:369
  54.2 2.3 %collective-permute-start.8 = (s16[32,2176]{1,0:T(8,128)(2,1)S(1)}, s16[32,2176]{1,0:T(8,128)(2,1)S(1)}, u32[]{:S(2)}, u32[]{:S(2)}) collective-permute-start(s16[32,2176]{1,0:T(8,128)(2,1)S(1)} %get-tuple-element.34), channel_id=1, source_target_pairs={{0,240},{16,224},{32,208},{48,192},{64,176},{80,160},{96,144},{112... | collective-permute-start | bytes 417800 | tf_op jit(solution)/shard_map/ppermute | solution.py:369
  56.6 0.0 collective-permute-start.9
  56.6 0.0 collective-permute-start.10
  56.6 0.0 collective-permute-done.6.refs_1_
  56.6 2.6 %collective-permute-start.11 = (s16[32,2176]{1,0:T(8,128)(2,1)S(1)}, s16[32,2176]{1,0:T(8,128)(2,1)S(1)}, u32[]{:S(2)}, u32[]{:S(2)}) collective-permute-start(s16[32,2176]{1,0:T(8,128)(2,1)S(1)} %get-tuple-element.38), channel_id=1, source_target_pairs={{0,80},{16,64},{32,112},{48,96},{64,16},{80,0},{96,48},{112,32},{1... | collective-permute-start | bytes 417800 | tf_op jit(solution)/shard_map/ppermute | solution.py:369
  59.2 0.1 collective-permute-done.7.refs_2_
  59.3 3.8 %collective-permute-done.8.refs_3_ = s16[32,2176]{1,0:T(8,128)(2,1)S(1)} collective-permute-done((s16[32,2176]{1,0:T(8,128)(2,1)S(1)}, s16[32,2176]{1,0:T(8,128)(2,1)S(1)}, u32[]{:S(2)}, u32[]{:S(2)}) %collective-permute-start.8) | collective-permute-done | bytes 139296 | tf_op jit(solution)/shard_map/ppermute | solution.py:369
  63.0 1.1 %fold.2.refs_2_ = f32[16,2176]{1,0:T(8,128)S(1)} custom-call(f32[32,2176]{1,0:T(8,128)S(1)} %get-tuple-element.31.refs_0_, s16[32,2176]{1,0:T(8,128)(2,1)S(1)} %collective-permute-done.6.refs_1_, s16[32,2176]{1,0:T(8,128)(2,1)S(1)} %collective-permute-done.7.refs_2_, s16[32,2176]{1,0:T(8,128)(2,1)S(1)} %collective-permute-done.8.refs_3_), custom_call_target="tpu_custom_call" | custom-call | tf_op jit(solution)/shard_map/fold/pallas_call | solution.py:330
  64.2 0.0 collective-permute-done.9.refs_1_
  64.2 0.0 collective-permute-done.10.refs_2_
  64.2 0.1 collective-permute-done.11.refs_3_
  64.3 1.1 %fold.3.refs_3_ = f32[16,2176]{1,0:T(8,128)S(1)} custom-call(f32[32,2176]{1,0:T(8,128)S(1)} %get-tuple-element.35.refs_0_, s16[32,2176]{1,0:T(8,128)(2,1)S(1)} %collective-permute-done.9.refs_1_, s16[32,2176]{1,0:T(8,128)(2,1)S(1)} %collective-permute-done.10.refs_2_, s16[32,2176]{1,0:T(8,128)(2,1)S(1)} %collective-permute-done.11.refs_3_), custom_call_target="tpu_custom_call" | custom-call | tf_op jit(solution)/shard_map/fold/pallas_call | solution.py:330
  65.5 0.0 all-to-all-done
  65.5 0.0 copy-done
  65.5 1.5 %finish.1 = f32[16,2,2048]{2,1,0:T(2,128)} custom-call(s32[16]{0:T(128)S(1)} %copy-done, f32[256,128]{1,0:T(8,128)S(1)} %bitcast.7, f32[16,2176]{1,0:T(8,128)S(1)} %fold.2.refs_2_, f32[16,2176]{1,0:T(8,128)S(1)} %fold.3.refs_3_), custom_call_target="tpu_custom_call" | custom-call | tf_op jit(solution)/shard_map/finish/pallas_call | solution.py:358
Async XLA Ops:
  0.0 65.5 %copy-start = (s32[16]{0:T(128)S(1)}, s32[16]{0:T(128)}, u32[]{:S(2)}) copy-start(s32[16]{0:T(128)} %refs_0_.1) | copy-start | bytes 196
  10.2 8.8 %collective-permute-start = (s16[80,2176]{1,0:T(8,128)(2,1)S(1)}, s16[80,2176]{1,0:T(8,128)(2,1)S(1)}, u32[]{:S(2)}, u32[]{:S(2)}) collective-permute-start(s16[80,2176]{1,0:T(8,128)(2,1)S(1)} %get-tuple-element.24), channel_id=1, source_target_pairs={{0,64},{16,80},{32,96},{48,112},{64,0},{80,16},{96,32},{112,48},{1... | collective-permute-start | bytes 1044488 | tf_op jit(solution)/shard_map/ppermute | solution.py:369
  12.3 12.8 %collective-permute-start.1 = (s16[80,2176]{1,0:T(8,128)(2,1)S(1)}, s16[80,2176]{1,0:T(8,128)(2,1)S(1)}, u32[]{:S(2)}, u32[]{:S(2)}) collective-permute-start(s16[80,2176]{1,0:T(8,128)(2,1)S(1)} %get-tuple-element.25), channel_id=1, source_target_pairs={{0,16},{16,0},{32,48},{48,32},{64,80},{80,64},{96,112},{112,96},{1... | collective-permute-start | bytes 1044488 | tf_op jit(solution)/shard_map/ppermute | solution.py:369
  13.6 15.1 %collective-permute-start.2 = (s16[80,2176]{1,0:T(8,128)(2,1)S(1)}, s16[80,2176]{1,0:T(8,128)(2,1)S(1)}, u32[]{:S(2)}, u32[]{:S(2)}) collective-permute-start(s16[80,2176]{1,0:T(8,128)(2,1)S(1)} %get-tuple-element.26), channel_id=1, source_target_pairs={{0,80},{16,64},{32,112},{48,96},{64,16},{80,0},{96,48},{112,32},{1... | collective-permute-start | bytes 1044488 | tf_op jit(solution)/shard_map/ppermute | solution.py:369
  13.6 15.1 %collective-permute-start.3 = (s16[80,2176]{1,0:T(8,128)(2,1)S(1)}, s16[80,2176]{1,0:T(8,128)(2,1)S(1)}, u32[]{:S(2)}, u32[]{:S(2)}) collective-permute-start(s16[80,2176]{1,0:T(8,128)(2,1)S(1)} %get-tuple-element.28), channel_id=1, source_target_pairs={{0,192},{16,208},{32,224},{48,240},{64,128},{80,144},{96,160},{112... | collective-permute-start | bytes 1044488 | tf_op jit(solution)/shard_map/ppermute | solution.py:369
  16.3 12.4 %collective-permute-start.4 = (s16[80,2176]{1,0:T(8,128)(2,1)S(1)}, s16[80,2176]{1,0:T(8,128)(2,1)S(1)}, u32[]{:S(2)}, u32[]{:S(2)}) collective-permute-start(s16[80,2176]{1,0:T(8,128)(2,1)S(1)} %get-tuple-element.29), channel_id=1, source_target_pairs={{0,48},{16,32},{32,16},{48,0},{64,112},{80,96},{96,80},{112,64},{1... | collective-permute-start | bytes 1044488 | tf_op jit(solution)/shard_map/ppermute | solution.py:369
  19.0 12.7 %collective-permute-start.5 = (s16[80,2176]{1,0:T(8,128)(2,1)S(1)}, s16[80,2176]{1,0:T(8,128)(2,1)S(1)}, u32[]{:S(2)}, u32[]{:S(2)}) collective-permute-start(s16[80,2176]{1,0:T(8,128)(2,1)S(1)} %get-tuple-element.30), channel_id=1, source_target_pairs={{0,240},{16,224},{32,208},{48,192},{64,176},{80,160},{96,144},{112... | collective-permute-start | bytes 1044488 | tf_op jit(solution)/shard_map/ppermute | solution.py:369
  33.4 23.1 %collective-permute-start.6 = (s16[32,2176]{1,0:T(8,128)(2,1)S(1)}, s16[32,2176]{1,0:T(8,128)(2,1)S(1)}, u32[]{:S(2)}, u32[]{:S(2)}) collective-permute-start(s16[32,2176]{1,0:T(8,128)(2,1)S(1)} %get-tuple-element.32), channel_id=1, source_target_pairs={{0,192},{16,208},{32,224},{48,240},{64,128},{80,144},{96,160},{112... | collective-permute-start | bytes 417800 | tf_op jit(solution)/shard_map/ppermute | solution.py:369
  37.7 27.8 %all-to-all-start = ((f32[256,1,128]{2,1,0:T(1,128)}), f32[256,1,128]{2,1,0:T(1,128)S(1)}, u32[]{:S(2)}, u32[]{:S(2)}) async-start(f32[256,1,128]{2,1,0:T(1,128)} %bitcast.3), calls=%async_computation | async-start | bytes 262144 | tf_op jit(solution)/shard_map/all_to_all | solution.py:382
  51.5 7.8 %collective-permute-start.7 = (s16[32,2176]{1,0:T(8,128)(2,1)S(1)}, s16[32,2176]{1,0:T(8,128)(2,1)S(1)}, u32[]{:S(2)}, u32[]{:S(2)}) collective-permute-start(s16[32,2176]{1,0:T(8,128)(2,1)S(1)} %get-tuple-element.33), channel_id=1, source_target_pairs={{0,48},{16,32},{32,16},{48,0},{64,112},{80,96},{96,80},{112,64},{1... | collective-permute-start | bytes 417800 | tf_op jit(solution)/shard_map/ppermute | solution.py:369
  54.2 8.8 %collective-permute-start.8 = (s16[32,2176]{1,0:T(8,128)(2,1)S(1)}, s16[32,2176]{1,0:T(8,128)(2,1)S(1)}, u32[]{:S(2)}, u32[]{:S(2)}) collective-permute-start(s16[32,2176]{1,0:T(8,128)(2,1)S(1)} %get-tuple-element.34), channel_id=1, source_target_pairs={{0,240},{16,224},{32,208},{48,192},{64,176},{80,160},{96,144},{112... | collective-permute-start | bytes 417800 | tf_op jit(solution)/shard_map/ppermute | solution.py:369
  56.6 7.6 %collective-permute-start.9 = (s16[32,2176]{1,0:T(8,128)(2,1)S(1)}, s16[32,2176]{1,0:T(8,128)(2,1)S(1)}, u32[]{:S(2)}, u32[]{:S(2)}) collective-permute-start(s16[32,2176]{1,0:T(8,128)(2,1)S(1)} %get-tuple-element.36), channel_id=1, source_target_pairs={{0,64},{16,80},{32,96},{48,112},{64,0},{80,16},{96,32},{112,48},{1... | collective-permute-start | bytes 417800 | tf_op jit(solution)/shard_map/ppermute | solution.py:369
  56.6 7.6 %collective-permute-start.10 = (s16[32,2176]{1,0:T(8,128)(2,1)S(1)}, s16[32,2176]{1,0:T(8,128)(2,1)S(1)}, u32[]{:S(2)}, u32[]{:S(2)}) collective-permute-start(s16[32,2176]{1,0:T(8,128)(2,1)S(1)} %get-tuple-element.37), channel_id=1, source_target_pairs={{0,16},{16,0},{32,48},{48,32},{64,80},{80,64},{96,112},{112,96},{1... | collective-permute-start | bytes 417800 | tf_op jit(solution)/shard_map/ppermute | solution.py:369
  56.6 7.7 %collective-permute-start.11 = (s16[32,2176]{1,0:T(8,128)(2,1)S(1)}, s16[32,2176]{1,0:T(8,128)(2,1)S(1)}, u32[]{:S(2)}, u32[]{:S(2)}) collective-permute-start(s16[32,2176]{1,0:T(8,128)(2,1)S(1)} %get-tuple-element.38), channel_id=1, source_target_pairs={{0,80},{16,64},{32,112},{48,96},{64,16},{80,0},{96,48},{112,32},{1... | collective-permute-start | bytes 417800 | tf_op jit(solution)/shard_map/ppermute | solution.py:369
